TPU v7x, 256 devices: a whole 4x4x8 slice. The times are simulated.
256 devices in a mesh: ha: 8 (over z_lo, core), wa: 32 (over y, x, z_hi).
Axes of the slice: x: 4, y: 4, z: 8 (z_hi: 2, z_lo: 4; z = z_hi * 4 + z_lo), core: 2. Of those that a mesh axis runs over, the one named last changes fastest.
Arguments:
- tokens: bfloat16 [1, 8, 64, 64, 1152], P(None, None, 'ha', 'wa'), may hold values from -36 to 36
- cotangent: bfloat16 [1, 8, 64, 64, 1152], P(None, None, 'ha', 'wa'), may hold values from -6 to 6
- w_qkv: bfloat16 [3, 1152, 1728], P(None, 'wa'), may hold values from -0.1875 to 0.1875
- w_out: bfloat16 [3, 576, 1152], P(None, 'wa'), may hold values from -0.25 to 0.25
- gains: float32 [3, 1152], replicated, may hold values from 0.1 to 1.9
- gates: float32 [3, 8], replicated, may hold values from 0.5 to 2
Outputs:
- token_grad: bfloat16 [1, 8, 64, 64, 1152], P(None, None, 'ha', 'wa')
- head_sens: bfloat16 [1, 3, 8, 64, 64, 8], P(None, None, None, 'ha', 'wa')
All inputs are finite; a program needn't handle non-finite values.
Results may differ from a plain program's by a relative error of at most 0.02.
Values may be sent and summed in bfloat16 or wider, within the bound.
A program may use at most 128 MiB of HBM per device.

v0:
```python
import jax
import jax.numpy as jnp
from jax import lax
from jax.sharding import PartitionSpec as P


def letter_forms(attend_axis):
    letters = "bfhw"
    query_side = letters + "nc"
    key_side = letters[:attend_axis] + "g" + letters[attend_axis + 1 :] + "nc"
    score_side = (
        letters[:attend_axis] + letters[attend_axis + 1 :] + "n" + letters[attend_axis] + "g"
    )
    return (
        query_side + "," + key_side + "->" + score_side,
        score_side + "," + key_side + "->" + query_side,
        score_side + "," + query_side + "->" + key_side,
    )


def product(form, left, right):
    return jnp.einsum(form, left, right, preferred_element_type=jnp.float32)


def forward_sublayer(inputs, w_qkv, w_out, gain, gate, attend_axis, keep_output):
    scores_form, mixing_form, keyward_form = letter_forms(attend_axis)
    heads = gate.shape[0]
    hidden = w_out.shape[0]
    head_dim = hidden // heads
    leading = inputs.shape[:4]
    inputs_f = inputs.astype(jnp.float32)
    inverse = lax.rsqrt(jnp.mean(inputs_f * inputs_f, axis=-1, keepdims=True) + 1e-06)
    normed = (inputs_f * inverse * gain).astype(jnp.bfloat16)
    projected = jnp.dot(normed, w_qkv, preferred_element_type=jnp.float32).astype(jnp.bfloat16)
    split = projected.reshape(leading + (3, heads, head_dim))
    queries = split[..., 0, :, :]
    keys_all = split[..., 1, :, :]
    values = split[..., 2, :, :]
    scores = product(scores_form, queries, keys_all) * head_dim ** (-0.5)
    raised = jnp.exp(scores)
    probs = raised / jnp.sum(raised, axis=-1, keepdims=True)
    probs_half = probs.astype(jnp.bfloat16)
    attended = product(mixing_form, probs_half, values).astype(jnp.bfloat16)
    saved = (inverse, queries, keys_all, values, probs, probs_half, attended)
    if not keep_output:
        return (inputs, saved)
    gated = (
        (attended.astype(jnp.float32) * gate[:, None])
        .astype(jnp.bfloat16)
        .reshape(leading + (hidden,))
    )
    outputs = (inputs_f + jnp.dot(gated, w_out, preferred_element_type=jnp.float32)).astype(
        jnp.bfloat16
    )
    return (outputs, saved)


def backward_sublayer(outgrad, inputs, saved, w_qkv, w_out, gain, gate, attend_axis):
    scores_form, mixing_form, keyward_form = letter_forms(attend_axis)
    inverse, queries, keys_all, values, probs, probs_half, attended = saved
    heads = gate.shape[0]
    hidden = w_out.shape[0]
    head_dim = hidden // heads
    leading = inputs.shape[:4]
    d_gated = jnp.dot(outgrad, w_out.T, preferred_element_type=jnp.float32).astype(jnp.bfloat16)
    d_gated = d_gated.reshape(leading + (heads, head_dim))
    sens = jnp.sum(d_gated.astype(jnp.float32) * attended.astype(jnp.float32), axis=-1).astype(
        jnp.bfloat16
    )
    d_attended = (d_gated.astype(jnp.float32) * gate[:, None]).astype(jnp.bfloat16)
    d_probs = product(scores_form, d_attended, values)
    d_values = product(keyward_form, probs_half, d_attended)
    d_scores = (
        probs * (d_probs - jnp.sum(d_probs * probs, axis=-1, keepdims=True)) * head_dim ** (-0.5)
    ).astype(jnp.bfloat16)
    d_queries = product(mixing_form, d_scores, keys_all)
    d_keys = product(keyward_form, d_scores, queries)
    d_proj = (
        jnp.stack([d_queries, d_keys, d_values], axis=4)
        .reshape(leading + (3 * hidden,))
        .astype(jnp.bfloat16)
    )
    d_normed = jnp.dot(d_proj, w_qkv.T, preferred_element_type=jnp.float32) * gain
    inputs_f = inputs.astype(jnp.float32)
    ingrad = (
        outgrad.astype(jnp.float32)
        + inverse * d_normed
        - inputs_f
        * inverse
        * inverse
        * inverse
        * jnp.mean(inputs_f * d_normed, axis=-1, keepdims=True)
    )
    return (ingrad.astype(jnp.bfloat16), sens)


def per_device(tokens, cotangent, w_qkv, w_out, gains, gates):
    heads = gates.shape[1]

    def weights_for(sublayer):
        return (
            lax.all_gather(w_qkv[sublayer], "wa", axis=0, tiled=True),
            lax.all_gather(w_out[sublayer], "wa", axis=0, tiled=True),
        )

    qkv_first, out_first = weights_for(0)
    after_time, saved_time = forward_sublayer(
        tokens, qkv_first, out_first, gains[0], gates[0], 1, True
    )
    qkv_second, out_second = weights_for(1)
    tall_input = lax.all_to_all(after_time, "ha", split_axis=1, concat_axis=2, tiled=True)
    after_height, saved_height = forward_sublayer(
        tall_input, qkv_second, out_second, gains[1], gates[1], 2, True
    )
    qkv_third, out_third = weights_for(2)
    wide_input = lax.all_to_all(after_height, "wa", split_axis=2, concat_axis=3, tiled=True)
    wide_same, saved_width = forward_sublayer(
        wide_input, qkv_third, out_third, gains[2], gates[2], 3, False
    )
    tall_cot = lax.all_to_all(cotangent, "ha", split_axis=1, concat_axis=2, tiled=True)
    wide_cot = lax.all_to_all(tall_cot, "wa", split_axis=2, concat_axis=3, tiled=True)
    grad_width, sens_width = backward_sublayer(
        wide_cot, wide_input, saved_width, qkv_third, out_third, gains[2], gates[2], 3
    )
    tall_grad, tall_sens = (
        lax.all_to_all(grad_width, "wa", split_axis=3, concat_axis=2, tiled=True),
        lax.all_to_all(sens_width, "wa", split_axis=3, concat_axis=2, tiled=True),
    )
    grad_height, sens_height = backward_sublayer(
        tall_grad, tall_input, saved_height, qkv_second, out_second, gains[1], gates[1], 2
    )
    home_cot, both_sens = (
        lax.all_to_all(grad_height, "ha", split_axis=2, concat_axis=1, tiled=True),
        lax.all_to_all(
            jnp.concatenate([tall_sens, sens_height], axis=-1),
            "ha",
            split_axis=2,
            concat_axis=1,
            tiled=True,
        ),
    )
    home_sens_width = both_sens[..., :heads]
    home_sens_height = both_sens[..., heads:]
    token_grad, sens_time = backward_sublayer(
        home_cot, tokens, saved_time, qkv_first, out_first, gains[0], gates[0], 1
    )
    head_sens = jnp.stack([sens_time, home_sens_height, home_sens_width], axis=1)
    return (token_grad, head_sens)


def solution(mesh):
    in_specs = (
        P(None, None, "ha", "wa", None),
        P(None, None, "ha", "wa", None),
        P(None, "wa", None),
        P(None, "wa", None),
        P(),
        P(),
    )
    out_specs = (P(None, None, "ha", "wa", None), P(None, None, None, "ha", "wa", None))
    return jax.shard_map(
        per_device, mesh=mesh, in_specs=in_specs, out_specs=out_specs, check_vma=False
    )
```

profile of v0, /device:TPU:1, one launch (start us, length us, event | category | flops | bytes accessed | tf_op | source)
XLA Modules:
  0.0 885.5 jit_solution(4877952526610603117)
XLA Ops:
  14.5 7.4 all-to-all-start
  22.7 145.0 %all-gather.13.cloned.1.call-done = bf16[1,1152,1728]{2,0,1:T(2,128)(2,1)} async-done(((bf16[1,36,1728]{2,0,1:T(2,128)(2,1)}), bf16[1,1152,1728]{2,0,1:T(2,128)(2,1)}) %all-gather.13.cloned.1.call-update) | async-done | bytes 3981328 | tf_op jit(solution)/shard_map/all_gather | solution.py:102
  167.7 17.9 %copy.441 = bf16[1,1152,1728]{1,2,0:T(8,128)(2,1)} copy(bf16[1,1152,1728]{2,0,1:T(2,128)(2,1)} %all-gather.13.cloned.1.call-done) | data formatting | bytes 7962624 | tf_op jit(solution)/shard_map/all_gather | solution.py:102
  185.5 3.4 fusion.31
  191.9 66.3 %all-gather.15.cloned.1.call-done = bf16[1,576,1152]{2,0,1:T(2,128)(2,1)} async-done(((bf16[1,18,1152]{2,0,1:T(2,128)(2,1)}), bf16[1,576,1152]{2,0,1:T(2,128)(2,1)}) %all-gather.15.cloned.1.call-update) | async-done | bytes 1327120 | tf_op jit(solution)/shard_map/all_gather | solution.py:103
  261.1 8.8 all-to-all-start.2
  269.9 142.3 %all-gather.17.cloned.1.call-done = bf16[1,1152,1728]{2,0,1:T(2,128)(2,1)} async-done(((bf16[1,36,1728]{2,0,1:T(2,128)(2,1)}), bf16[1,1152,1728]{2,0,1:T(2,128)(2,1)}) %all-gather.17.cloned.1.call-update) | async-done | bytes 3981328 | tf_op jit(solution)/shard_map/all_gather | solution.py:102
  412.3 17.8 %copy.453 = bf16[1,1152,1728]{1,2,0:T(8,128)(2,1)} copy(bf16[1,1152,1728]{2,0,1:T(2,128)(2,1)} %all-gather.17.cloned.1.call-done) | data formatting | bytes 7962624 | tf_op jit(solution)/shard_map/all_gather | solution.py:102
  430.1 5.4 all-to-all-start.1
  435.7 3.4 fusion.25
  442.0 60.2 %all-gather.19.cloned.1.call-done = bf16[1,576,1152]{2,0,1:T(2,128)(2,1)} async-done(((bf16[1,18,1152]{2,0,1:T(2,128)(2,1)}), bf16[1,576,1152]{2,0,1:T(2,128)(2,1)}) %all-gather.19.cloned.1.call-update) | async-done | bytes 1327120 | tf_op jit(solution)/shard_map/all_gather | solution.py:103
  505.4 5.5 all-to-all-start.3
  512.2 84.0 %all-gather.23.cloned.1.call-done = bf16[1,576,1152]{2,0,1:T(2,128)(2,1)} async-done(((bf16[1,18,1152]{2,0,1:T(2,128)(2,1)}), bf16[1,576,1152]{2,0,1:T(2,128)(2,1)}) %all-gather.23.cloned.1.call-update) | async-done | bytes 1327120 | tf_op jit(solution)/shard_map/all_gather | solution.py:103
  599.9 150.2 %all-gather.21.cloned.1.call-done = bf16[1,1152,1728]{2,0,1:T(2,128)(2,1)} async-done(((bf16[1,36,1728]{2,0,1:T(2,128)(2,1)}), bf16[1,1152,1728]{2,0,1:T(2,128)(2,1)}) %all-gather.21.cloned.1.call-update) | async-done | bytes 3981328 | tf_op jit(solution)/shard_map/all_gather | solution.py:102
  750.1 17.8 %copy.465 = bf16[1,1152,1728]{1,2,0:T(8,128)(2,1)} copy(bf16[1,1152,1728]{2,0,1:T(2,128)(2,1)} %all-gather.21.cloned.1.call-done) | data formatting | bytes 7962624 | tf_op jit(solution)/shard_map/all_gather | solution.py:102
  769.0 4.2 fusion.28
  786.8 5.4 all-to-all-start.6
  797.8 5.5 all-to-all-done.6
  803.3 6.1 all-to-all-start.4
  810.3 11.6 %all-to-all-done.4 = bf16[1,1,2,64,1152]{4,2,1,0,3:T(2,128)(2,1)S(1)} async-done(((bf16[1,1,2,64,1152]{4,2,1,0,3:T(2,128)(2,1)}), bf16[1,1,2,64,1152]{4,2,1,0,3:T(2,128)(2,1)S(1)}, u32[]{:S(2)}, u32[]{:S(2)}) %all-to-all-start.4) | async-done | bytes 294944 | tf_op jit(solution)/shard_map/all_to_all | solution.py:126
  822.9 3.1 fusion.85
  836.0 8.8 all-to-all-start.7
  850.4 5.1 all-to-all-start.5
  855.9 8.9 %all-to-all-done.5 = bf16[1,1,64,2,1152]{4,3,1,0,2:T(2,128)(2,1)S(1)} async-done(((bf16[1,1,64,2,1152]{4,3,1,0,2:T(2,128)(2,1)}), bf16[1,1,64,2,1152]{4,3,1,0,2:T(2,128)(2,1)S(1)}, u32[]{:S(2)}, u32[]{:S(2)}) %all-to-all-start.5) | async-done | bytes 294944 | tf_op jit(solution)/shard_map/all_to_all | solution.py:133
  (180 shorter events, 76.3 us)
Async XLA Ops:
  7.2 160.5 %all-gather.13.cloned.1.call-start = ((), (), s32[]{:S(2)}) async-start(), calls=%async_computation.8 | async-start | bytes 8515584 | tf_op jit(solution)/shard_map/all_gather | solution.py:102
  9.3 249.0 %all-gather.15.cloned.1.call-start = ((), (), s32[]{:S(2)}) async-start(), calls=%async_computation.9 | async-start | bytes 2737152 | tf_op jit(solution)/shard_map/all_gather | solution.py:103
  10.9 401.3 %all-gather.17.cloned.1.call-start = ((), (), s32[]{:S(2)}) async-start(), calls=%async_computation.10 | async-start | bytes 8515584 | tf_op jit(solution)/shard_map/all_gather | solution.py:102
  12.0 490.3 %all-gather.19.cloned.1.call-start = ((), (), s32[]{:S(2)}) async-start(), calls=%async_computation.11 | async-start | bytes 2737152 | tf_op jit(solution)/shard_map/all_gather | solution.py:103
  12.7 583.5 %all-gather.23.cloned.1.call-start = ((), (), s32[]{:S(2)}) async-start(), calls=%async_computation.13 | async-start | bytes 2737152 | tf_op jit(solution)/shard_map/all_gather | solution.py:103
  13.5 736.6 %all-gather.21.cloned.1.call-start = ((), (), s32[]{:S(2)}) async-start(), calls=%async_computation.12 | async-start | bytes 8515584 | tf_op jit(solution)/shard_map/all_gather | solution.py:102
  14.5 246.7 %all-to-all-start = ((bf16[1,8,8,2,1152]{4,3,2,0,1:T(2,128)(2,1)}), bf16[1,8,8,2,1152]{4,3,2,0,1:T(2,128)(2,1)}, u32[]{:S(2)}, u32[]{:S(2)}) async-start(bf16[1,8,8,2,1152]{4,3,2,0,1:T(2,128)(2,1)} %bitcast.371), calls=%async_computation | async-start | bytes 589824 | tf_op jit(solution)/shard_map/all_to_all | solution.py:120
  21.9 163.6 %copy-start.19 = (f32[1152]{0:T(1024)}, f32[1152]{0:T(1024)S(1)}, u32[]{:S(2)}) copy-start(f32[1152]{0:T(1024)S(1)} %get-tuple-element.21) | copy-start | bytes 13828
  22.6 167.9 %copy-start.26 = (f32[8]{0:T(128)}, f32[8]{0:T(128)S(1)}, u32[]{:S(2)}) copy-start(f32[8]{0:T(128)S(1)} %get-tuple-element.41) | copy-start | bytes 100
  22.6 162.9 %copy-start.17 = (f32[8,8,2]{1,2,0:T(2,128)}, f32[8,8,2]{1,2,0:T(2,128)S(1)}, u32[]{:S(2)}) copy-start(f32[8,8,2]{1,2,0:T(2,128)S(1)} %add_rsqrt_fusion.2) | copy-start | bytes 1540
  190.0 71.1 %copy-start.14 = (bf16[1,8,8,2,1,8,72]{6,5,4,2,3,1,0:T(8,128)(2,1)}, bf16[1,8,8,2,1,8,72]{6,5,4,2,3,1,0:T(8,128)(2,1)S(1)}, u32[]{:S(2)}) copy-start(bf16[1,8,8,2,1,8,72]{6,5,4,2,3,1,0:T(8,128)(2,1)S(1)} %get-tuple-element.31) | copy-start | bytes 442372
  261.1 168.9 %all-to-all-start.2 = ((bf16[1,8,8,2,1152]{4,2,3,0,1:T(8,128)(2,1)}), bf16[1,8,8,2,1152]{4,2,3,0,1:T(8,128)(2,1)S(1)}, u32[]{:S(2)}, u32[]{:S(2)}) async-start(bf16[1,8,8,2,1152]{4,2,3,0,1:T(8,128)(2,1)} %fusion.37), calls=%async_computation.2 | async-start | bytes 589824 | tf_op jit(solution)/shard_map/all_to_all | solution.py:111
  430.1 75.3 %all-to-all-start.1 = ((bf16[1,1,64,2,1152]{4,3,1,0,2:T(2,128)(2,1)}), bf16[1,1,64,2,1152]{4,3,1,0,2:T(2,128)(2,1)}, u32[]{:S(2)}, u32[]{:S(2)}) async-start(bf16[1,1,64,2,1152]{4,3,1,0,2:T(2,128)(2,1)} %bitcast.2), calls=%async_computation.1 | async-start | bytes 589824 | tf_op jit(solution)/shard_map/all_to_all | solution.py:121
  440.2 65.3 %copy-start.1 = (bf16[1,1,64,2,1,8,72]{6,5,4,2,3,1,0:T(8,128)(2,1)}, bf16[1,1,64,2,1,8,72]{6,5,4,2,3,1,0:T(8,128)(2,1)S(1)}, u32[]{:S(2)}) copy-start(bf16[1,1,64,2,1,8,72]{6,5,4,2,3,1,0:T(8,128)(2,1)S(1)} %get-tuple-element.26) | copy-start | bytes 442372
  440.2 65.3 %copy-start.15 = (bf16[1,1,64,2,1,8,72]{6,5,4,2,3,1,0:T(8,128)(2,1)}, bf16[1,1,64,2,1,8,72]{6,5,4,2,3,1,0:T(8,128)(2,1)S(1)}, u32[]{:S(2)}) copy-start(bf16[1,1,64,2,1,8,72]{6,5,4,2,3,1,0:T(8,128)(2,1)S(1)} %get-tuple-element.27) | copy-start | bytes 442372
  440.2 65.3 %copy-start.16 = (bf16[1,1,64,2,1,8,72]{6,5,4,2,3,1,0:T(8,128)(2,1)}, bf16[1,1,64,2,1,8,72]{6,5,4,2,3,1,0:T(8,128)(2,1)S(1)}, u32[]{:S(2)}) copy-start(bf16[1,1,64,2,1,8,72]{6,5,4,2,3,1,0:T(8,128)(2,1)S(1)} %get-tuple-element.28) | copy-start | bytes 442372
  440.5 64.9 %copy-start.3 = (f32[2,8,64,64]{2,3,1,0:T(8,128)}, f32[2,8,64,64]{2,3,1,0:T(8,128)S(1)}, u32[]{:S(2)}) copy-start(f32[2,8,64,64]{2,3,1,0:T(8,128)S(1)} %fusion.155) | copy-start | bytes 786436
  505.4 262.4 %all-to-all-start.3 = ((bf16[1,1,64,2,1152]{4,3,1,0,2:T(2,128)(2,1)}), bf16[1,1,64,2,1152]{4,3,1,0,2:T(2,128)(2,1)S(1)}, u32[]{:S(2)}, u32[]{:S(2)}) async-start(bf16[1,1,64,2,1152]{4,3,1,0,2:T(2,128)(2,1)} %copy.460), calls=%async_computation.3 | async-start | bytes 589824 | tf_op jit(solution)/shard_map/all_to_all | solution.py:116
  512.2 255.7 %copy-start.7 = (bf16[2,64,1152]{2,1,0:T(8,128)(2,1)}, bf16[2,64,1152]{2,1,0:T(8,128)(2,1)S(1)}, u32[]{:S(2)}) copy-start(bf16[2,64,1152]{2,1,0:T(8,128)(2,1)S(1)} %all_to_all.85) | copy-start | bytes 884740
  786.8 16.5 %all-to-all-start.6 = ((bf16[1,1,2,64,8]{4,2,1,0,3:T(2,128)(2,1)}), bf16[1,1,2,64,8]{4,2,1,0,3:T(2,128)(2,1)}, u32[]{:S(2)}, u32[]{:S(2)}) async-start(bf16[1,1,2,64,8]{4,2,1,0,3:T(2,128)(2,1)} %copy.488), calls=%async_computation.6 | async-start | bytes 65536 | tf_op jit(solution)/shard_map/all_to_all | solution.py:127
  796.8 33.7 %copy-start.4 = (f32[2,8,64,64]{2,3,1,0:T(8,128)S(1)}, f32[2,8,64,64]{2,3,1,0:T(8,128)}, u32[]{:S(2)}) copy-start(f32[2,8,64,64]{2,3,1,0:T(8,128)} %copy-done.3) | copy-start | bytes 786436
  803.3 18.6 %all-to-all-start.4 = ((bf16[1,1,2,64,1152]{4,2,1,0,3:T(2,128)(2,1)}), bf16[1,1,2,64,1152]{4,2,1,0,3:T(2,128)(2,1)S(1)}, u32[]{:S(2)}, u32[]{:S(2)}) async-start(bf16[1,1,2,64,1152]{4,2,1,0,3:T(2,128)(2,1)} %copy.473), calls=%async_computation.4 | async-start | bytes 589824 | tf_op jit(solution)/shard_map/all_to_all | solution.py:126
  836.0 14.4 %all-to-all-start.7 = ((bf16[8,2,128]{2,1,0:T(2,128)(2,1)}), bf16[8,2,128]{2,1,0:T(2,128)(2,1)S(1)}, u32[]{:S(2)}, u32[]{:S(2)}) async-start(bf16[8,2,128]{2,1,0:T(2,128)(2,1)} %reshape.584), calls=%async_computation.7 | async-start | bytes 8192 | tf_op jit(solution)/shard_map/all_to_all | solution.py:134
  850.4 14.4 %all-to-all-start.5 = ((bf16[1,1,64,2,1152]{4,3,1,0,2:T(2,128)(2,1)}), bf16[1,1,64,2,1152]{4,3,1,0,2:T(2,128)(2,1)S(1)}, u32[]{:S(2)}, u32[]{:S(2)}) async-start(bf16[1,1,64,2,1152]{4,3,1,0,2:T(2,128)(2,1)} %copy.478), calls=%async_computation.5 | async-start | bytes 589824 | tf_op jit(solution)/shard_map/all_to_all | solution.py:133
  (21 other events, 177.5 us)
Sparse Core Ops, SparseCore 0:
  12.1 155.5 all-gather.12
  171.6 86.6 all-gather.14
  261.8 150.4 all-gather.16
  415.5 86.6 all-gather.18
  505.5 90.7 all-gather.22
  599.6 150.4 all-gather.20
where the time goes:
time: 888 us; the launch traced here: 885 us
  waiting for transfers between devices  674 us (76%)
  local copies, waits for them, and re-layouts  86.3 us (10%)
  matrix products  53.3 us (6%)
  starting transfers between devices  52.7 us (6%)
  between operations  14.9 us (2%)
    all_gather x3, waiting for transfers between devices, weights_for(): lax.all_gather(w_qkv[sublayer], 'wa', axis=0, tiled=True)  438 us
    all_gather x3, waiting for transfers between devices, weights_for(): lax.all_gather(w_out[sublayer], 'wa', axis=0, tiled=True)  211 us
    all_gather x3, local copies, waits for them, and re-layouts, weights_for(): lax.all_gather(w_qkv[sublayer], 'wa', axis=0, tiled=True)  53.5 us
    dot_general x15, matrix products, product(): return jnp.einsum(form, left, right, preferred_element_type=jnp.float32)  18.4 us
  transfers between devices with their start and end apart: 14, of which 9 were waited for; matrix products, arithmetic and copies ran while one was open for 11% of the time, Pallas kernels for 0%

commit v1 on v0

--- a/solution.py
+++ b/solution.py
@@ -2,6 +2,11 @@
 import jax.numpy as jnp
 from jax import lax
 from jax.sharding import PartitionSpec as P
+
+
+def all_by_exchange(value, axis, d):
+    sent = jnp.stack([value] * lax.axis_size(axis))
+    return jnp.concatenate(lax.all_to_all(sent, axis, 0, 0), axis=d)
 
 
 def letter_forms(attend_axis):
@@ -99,7 +104,7 @@
 
     def weights_for(sublayer):
         return (
-            lax.all_gather(w_qkv[sublayer], "wa", axis=0, tiled=True),
+            all_by_exchange(w_qkv[sublayer], "wa", 0),
             lax.all_gather(w_out[sublayer], "wa", axis=0, tiled=True),
         )
 

time: 888 us -> 734 us (0.83)
  waiting for transfers between devices: 674 us -> 395 us
  blocking collectives: 0 us -> 144 us
  local copies, waits for them, and re-layouts: 86.3 us -> 57 us
    all_gather x3 -> x0, waiting for transfers between devices: 438 us -> none  [weights_for(): lax.all_gather(w_qkv[sublayer], 'wa', axis=0, tiled=True)]
    all_gather x3, waiting for transfers between devices: 211 us -> 361 us  [weights_for(): lax.all_gather(w_out[sublayer], 'wa', axis=0, tiled=True)]
    all_to_all x0 -> x3, blocking collectives: none -> 144 us  [the longest x1 109 us: all_by_exchange(): return jnp.concatenate(lax.all_to_all(sent, axis, 0, 0), axis=d)]
    all_gather x3 -> x0, local copies, waits for them, and re-layouts: 53.5 us -> none  [weights_for(): lax.all_gather(w_qkv[sublayer], 'wa', axis=0, tiled=True)]
    reshape x0 -> x3, local copies, waits for them, and re-layouts: none -> 21.9 us  [all_by_exchange(): return jnp.concatenate(lax.all_to_all(sent, axis, 0, 0), axis=d)]
    all_to_all x1, waiting for transfers between devices: 0.01 us -> 11.9 us  [per_device(): lax.all_to_all(tall_cot, 'wa', split_axis=2, concat_axis=3, tiled=True)]
  transfers between devices with their start and end apart: 14 -> 11, of which waited for: 9 -> 7; matrix products, arithmetic and copies ran while one was open for 11% -> 9% of each run, Pallas kernels for 0% -> 0%
where the time goes in v1:
time: 734 us; the launch traced here: 732 us
  waiting for transfers between devices  395 us (54%)
  blocking collectives  144 us (20%)
  starting transfers between devices  58.9 us (8%)
  local copies, waits for them, and re-layouts  57 us (8%)
  matrix products  54 us (7%)
  between operations  14.5 us (2%)
  other arithmetic  8.56 us (1%)
    all_gather x3, waiting for transfers between devices, weights_for(): lax.all_gather(w_out[sublayer], 'wa', axis=0, tiled=True)  361 us
    all_to_all x1, blocking collectives, all_by_exchange(): return jnp.concatenate(lax.all_to_all(sent, axis, 0, 0), axis=d)  109 us
    reshape x3, local copies, waits for them, and re-layouts, all_by_exchange(): return jnp.concatenate(lax.all_to_all(sent, axis, 0, 0), axis=d)  21.9 us
    dot_general x15, matrix products, product(): return jnp.einsum(form, left, right, preferred_element_type=jnp.float32)  19.7 us
    all_to_all x1, blocking collectives, per_device(): lax.all_to_all(after_time, 'ha', split_axis=1, concat_axis=2, tiled=True)  17.7 us
    all_to_all x1, blocking collectives, per_device(): lax.all_to_all(cotangent, 'ha', split_axis=1, concat_axis=2, tiled=True)  17.3 us
  transfers between devices with their start and end apart: 11, of which 7 were waited for; matrix products, arithmetic and copies ran while one was open for 9% of the time, Pallas kernels for 0%

profile of v1, /device:TPU:1, one launch (start us, length us, event | category | flops | bytes accessed | tf_op | source)
XLA Modules:
  0.0 732.0 jit_solution(14964944528584324870)
XLA Ops:
  7.2 17.3 %all_to_all.123 = bf16[1,8,8,2,1152]{4,3,2,0,1:T(2,128)(2,1)} all-to-all(bf16[1,8,8,2,1152]{4,3,2,0,1:T(2,128)(2,1)} %bitcast.379), channel_id=1, replica_groups=mesh['ha'=8,'wa'=32] {'ha'}, dimensions={1} | all-to-all | bytes 589824 | tf_op jit(solution)/shard_map/all_to_all | solution.py:125
  24.5 11.7 %all-to-all-start.1 = ((bf16[1,1,64,2,1152]{4,3,1,0,2:T(2,128)(2,1)}), bf16[1,1,64,2,1152]{4,3,1,0,2:T(2,128)(2,1)S(1)}, u32[]{:S(2)}, u32[]{:S(2)}) async-start(bf16[1,1,64,2,1152]{4,3,1,0,2:T(2,128)(2,1)} %bitcast.2), calls=%async_computation.1 | async-start | bytes 589824 | tf_op jit(solution)/shard_map/all_to_all | solution.py:126
  37.3 11.9 %all-to-all-done.1 = bf16[1,1,64,2,1152]{4,3,1,0,2:T(2,128)(2,1)S(1)} async-done(((bf16[1,1,64,2,1152]{4,3,1,0,2:T(2,128)(2,1)}), bf16[1,1,64,2,1152]{4,3,1,0,2:T(2,128)(2,1)S(1)}, u32[]{:S(2)}, u32[]{:S(2)}) %all-to-all-start.1) | async-done | bytes 294944 | tf_op jit(solution)/shard_map/all_to_all | solution.py:126
  49.5 108.9 %all_to_all.124 = bf16[32,36,1728]{2,1,0:T(8,128)(2,1)} all-to-all(bf16[32,36,1728]{2,1,0:T(8,128)(2,1)S(1)} %stack.55), channel_id=1, replica_groups=mesh['ha'=8,'wa'=32] {'wa'}, dimensions={0} | all-to-all | bytes 7962624 | tf_op jit(solution)/shard_map/all_to_all | solution.py:9
  160.9 5.5 all-to-all-start.4
  168.7 7.3 reshape.707
  182.1 135.3 %all-gather.7.cloned.1.call-done = bf16[1,576,1152]{2,0,1:T(2,128)(2,1)} async-done(((bf16[1,18,1152]{2,0,1:T(2,128)(2,1)}), bf16[1,576,1152]{2,0,1:T(2,128)(2,1)}) %all-gather.7.cloned.1.call-update) | async-done | bytes 1327120 | tf_op jit(solution)/shard_map/all_gather | solution.py:108
  319.6 17.7 %all_to_all.125 = bf16[1,8,8,2,1152]{4,2,3,0,1:T(8,128)(2,1)S(1)} all-to-all(bf16[1,8,8,2,1152]{4,2,3,0,1:T(8,128)(2,1)S(1)} %fusion.37), channel_id=1, replica_groups=mesh['ha'=8,'wa'=32] {'ha'}, dimensions={1} | all-to-all | bytes 589824 | tf_op jit(solution)/shard_map/all_to_all | solution.py:116
  339.8 5.5 all-to-all-start.6
  346.8 7.3 reshape.713
  360.4 140.2 %all-gather.9.cloned.1.call-done = bf16[1,576,1152]{2,0,1:T(2,128)(2,1)} async-done(((bf16[1,18,1152]{2,0,1:T(2,128)(2,1)}), bf16[1,576,1152]{2,0,1:T(2,128)(2,1)}) %all-gather.9.cloned.1.call-update) | async-done | bytes 1327120 | tf_op jit(solution)/shard_map/all_gather | solution.py:108
  503.8 5.5 all-to-all-start.5
  509.7 85.0 %all-gather.11.cloned.1.call-done = bf16[1,576,1152]{2,0,1:T(2,128)(2,1)} async-done(((bf16[1,18,1152]{2,0,1:T(2,128)(2,1)}), bf16[1,576,1152]{2,0,1:T(2,128)(2,1)}) %all-gather.11.cloned.1.call-update) | async-done | bytes 1327120 | tf_op jit(solution)/shard_map/all_gather | solution.py:108
  598.3 7.3 reshape.719
  623.7 5.3 all-to-all-start.9
  631.2 3.7 multiply_reduce_fusion.3
  640.0 9.0 %all-to-all-start.7 = ((bf16[1,1,2,64,1152]{4,2,1,0,3:T(2,128)(2,1)}), bf16[1,1,2,64,1152]{4,2,1,0,3:T(2,128)(2,1)S(1)}, u32[]{:S(2)}, u32[]{:S(2)}) async-start(bf16[1,1,2,64,1152]{4,2,1,0,3:T(2,128)(2,1)} %copy.445), calls=%async_computation.7 | async-start | bytes 589824 | tf_op jit(solution)/shard_map/all_to_all | solution.py:131
  649.3 12.0 %all-to-all-done.7 = bf16[1,1,2,64,1152]{4,2,1,0,3:T(2,128)(2,1)S(1)} async-done(((bf16[1,1,2,64,1152]{4,2,1,0,3:T(2,128)(2,1)}), bf16[1,1,2,64,1152]{4,2,1,0,3:T(2,128)(2,1)S(1)}, u32[]{:S(2)}, u32[]{:S(2)}) %all-to-all-start.7) | async-done | bytes 294944 | tf_op jit(solution)/shard_map/all_to_all | solution.py:131
  662.3 3.1 fusion.85
  676.9 11.2 %all-to-all-start.10 = ((bf16[8,2,128]{2,1,0:T(2,128)(2,1)}), bf16[8,2,128]{2,1,0:T(2,128)(2,1)S(1)}, u32[]{:S(2)}, u32[]{:S(2)}) async-start(bf16[8,2,128]{2,1,0:T(2,128)(2,1)} %reshape.755), calls=%async_computation.10 | async-start | bytes 8192 | tf_op jit(solution)/shard_map/all_to_all | solution.py:139
  690.4 3.7 fusion.126
  696.3 5.1 all-to-all-start.8
  703.0 7.7 %all-to-all-done.8 = bf16[1,1,64,2,1152]{4,3,1,0,2:T(2,128)(2,1)S(1)} async-done(((bf16[1,1,64,2,1152]{4,3,1,0,2:T(2,128)(2,1)}), bf16[1,1,64,2,1152]{4,3,1,0,2:T(2,128)(2,1)S(1)}, u32[]{:S(2)}, u32[]{:S(2)}) %all-to-all-start.8) | async-done | bytes 294944 | tf_op jit(solution)/shard_map/all_to_all | solution.py:138
  720.4 3.7 fusion.131
  (183 shorter events, 86.5 us)
Async XLA Ops:
  24.5 24.7 %all-to-all-start.1 = ((bf16[1,1,64,2,1152]{4,3,1,0,2:T(2,128)(2,1)}), bf16[1,1,64,2,1152]{4,3,1,0,2:T(2,128)(2,1)S(1)}, u32[]{:S(2)}, u32[]{:S(2)}) async-start(bf16[1,1,64,2,1152]{4,3,1,0,2:T(2,128)(2,1)} %bitcast.2), calls=%async_computation.1 | async-start | bytes 589824 | tf_op jit(solution)/shard_map/all_to_all | solution.py:126
  160.9 158.7 %all-to-all-start.4 = ((bf16[32,36,1728]{2,1,0:T(8,128)(2,1)}), bf16[32,36,1728]{2,1,0:T(8,128)(2,1)}, u32[]{:S(2)}, u32[]{:S(2)}) async-start(bf16[32,36,1728]{2,1,0:T(8,128)(2,1)} %stack.56), calls=%async_computation.4 | async-start | bytes 9175040 | tf_op jit(solution)/shard_map/all_to_all | solution.py:9
  166.4 151.0 %all-gather.7.cloned.1.call-start = ((), (), s32[]{:S(2)}) async-start(), calls=%async_computation.11 | async-start | bytes 2737152 | tf_op jit(solution)/shard_map/all_gather | solution.py:108
  168.7 12.1 %copy-start.26 = (f32[8]{0:T(128)}, f32[8]{0:T(128)S(1)}, u32[]{:S(2)}) copy-start(f32[8]{0:T(128)S(1)} %get-tuple-element.39) | copy-start | bytes 100
  168.7 190.3 %copy-start.28 = (f32[8]{0:T(128)}, f32[8]{0:T(128)S(1)}, u32[]{:S(2)}) copy-start(f32[8]{0:T(128)S(1)} %get-tuple-element.40) | copy-start | bytes 100
  339.8 164.1 %all-to-all-start.6 = ((bf16[32,36,1728]{2,1,0:T(8,128)(2,1)}), bf16[32,36,1728]{2,1,0:T(8,128)(2,1)}, u32[]{:S(2)}, u32[]{:S(2)}) async-start(bf16[32,36,1728]{2,1,0:T(8,128)(2,1)} %stack.57), calls=%async_computation.6 | async-start | bytes 9175040 | tf_op jit(solution)/shard_map/all_to_all | solution.py:9
  345.3 155.4 %all-gather.9.cloned.1.call-start = ((), (), s32[]{:S(2)}) async-start(), calls=%async_computation.12 | async-start | bytes 2737152 | tf_op jit(solution)/shard_map/all_gather | solution.py:108
  346.0 248.6 %all-gather.11.cloned.1.call-start = ((), (), s32[]{:S(2)}) async-start(), calls=%async_computation.13 | async-start | bytes 2737152 | tf_op jit(solution)/shard_map/all_gather | solution.py:108
  358.3 145.6 %copy-start.2 = (bf16[1,1,64,2,1,8,72]{6,5,4,2,3,1,0:T(8,128)(2,1)}, bf16[1,1,64,2,1,8,72]{6,5,4,2,3,1,0:T(8,128)(2,1)S(1)}, u32[]{:S(2)}) copy-start(bf16[1,1,64,2,1,8,72]{6,5,4,2,3,1,0:T(8,128)(2,1)S(1)} %get-tuple-element.24) | copy-start | bytes 442372
  358.3 145.6 %copy-start.17 = (bf16[1,1,64,2,1,8,72]{6,5,4,2,3,1,0:T(8,128)(2,1)}, bf16[1,1,64,2,1,8,72]{6,5,4,2,3,1,0:T(8,128)(2,1)S(1)}, u32[]{:S(2)}) copy-start(bf16[1,1,64,2,1,8,72]{6,5,4,2,3,1,0:T(8,128)(2,1)S(1)} %get-tuple-element.26) | copy-start | bytes 442372
  358.6 238.4 %copy-start.4 = (f32[2,8,64,64]{2,3,1,0:T(8,128)}, f32[2,8,64,64]{2,3,1,0:T(8,128)S(1)}, u32[]{:S(2)}) copy-start(f32[2,8,64,64]{2,3,1,0:T(8,128)S(1)} %fusion.155) | copy-start | bytes 786436
  503.8 101.8 %all-to-all-start.5 = ((bf16[1,1,64,2,1152]{4,3,1,0,2:T(2,128)(2,1)}), bf16[1,1,64,2,1152]{4,3,1,0,2:T(2,128)(2,1)S(1)}, u32[]{:S(2)}, u32[]{:S(2)}) async-start(bf16[1,1,64,2,1152]{4,3,1,0,2:T(2,128)(2,1)} %copy.426), calls=%async_computation.5 | async-start | bytes 589824 | tf_op jit(solution)/shard_map/all_to_all | solution.py:121
  509.7 85.0 %copy-start.9 = (bf16[2,64,1152]{2,1,0:T(8,128)(2,1)}, bf16[2,64,1152]{2,1,0:T(8,128)(2,1)S(1)}, u32[]{:S(2)}) copy-start(bf16[2,64,1152]{2,1,0:T(8,128)(2,1)S(1)} %all_to_all.94) | copy-start | bytes 884740
  616.3 12.7 %copy-start.13 = (bf16[1,1,2,64,1,8,72]{6,3,5,2,4,1,0:T(8,128)(2,1)S(1)}, bf16[1,1,2,64,1,8,72]{6,3,5,2,4,1,0:T(8,128)(2,1)}, u32[]{:S(2)}) copy-start(bf16[1,1,2,64,1,8,72]{6,3,5,2,4,1,0:T(8,128)(2,1)} %fusion.70) | copy-start | bytes 442372
  623.7 16.3 %all-to-all-start.9 = ((bf16[1,1,2,64,8]{4,2,1,0,3:T(2,128)(2,1)}), bf16[1,1,2,64,8]{4,2,1,0,3:T(2,128)(2,1)S(1)}, u32[]{:S(2)}, u32[]{:S(2)}) async-start(bf16[1,1,2,64,8]{4,2,1,0,3:T(2,128)(2,1)} %copy.465), calls=%async_computation.9 | async-start | bytes 65536 | tf_op jit(solution)/shard_map/all_to_all | solution.py:132
  631.2 17.9 %copy-start.21 = (f32[8,8,2]{1,0,2:T(8,128)S(1)}, f32[8,8,2]{1,0,2:T(8,128)}, u32[]{:S(2)}) copy-start(f32[8,8,2]{1,0,2:T(8,128)} %copy-done.20) | copy-start | bytes 1540
  634.9 33.9 %copy-start.3 = (bf16[1,1,64,2,1,8,72]{6,5,4,2,3,1,0:T(8,128)(2,1)S(1)}, bf16[1,1,64,2,1,8,72]{6,5,4,2,3,1,0:T(8,128)(2,1)}, u32[]{:S(2)}) copy-start(bf16[1,1,64,2,1,8,72]{6,5,4,2,3,1,0:T(8,128)(2,1)} %copy-done.2) | copy-start | bytes 442372
  634.9 33.9 %copy-start.29 = (f32[8]{0:T(128)S(1)}, f32[8]{0:T(128)}, u32[]{:S(2)}) copy-start(f32[8]{0:T(128)} %copy-done.28) | copy-start | bytes 100
  636.2 33.7 %copy-start.5 = (f32[2,8,64,64]{2,3,1,0:T(8,128)S(1)}, f32[2,8,64,64]{2,3,1,0:T(8,128)}, u32[]{:S(2)}) copy-start(f32[2,8,64,64]{2,3,1,0:T(8,128)} %copy-done.4) | copy-start | bytes 786436
  640.0 21.3 %all-to-all-start.7 = ((bf16[1,1,2,64,1152]{4,2,1,0,3:T(2,128)(2,1)}), bf16[1,1,2,64,1152]{4,2,1,0,3:T(2,128)(2,1)S(1)}, u32[]{:S(2)}, u32[]{:S(2)}) async-start(bf16[1,1,2,64,1152]{4,2,1,0,3:T(2,128)(2,1)} %copy.445), calls=%async_computation.7 | async-start | bytes 589824 | tf_op jit(solution)/shard_map/all_to_all | solution.py:131
  662.3 12.5 %copy-start.8 = (f32[1,1,64,2,8,72]{5,2,4,3,1,0:T(8,128)S(1)}, f32[1,1,64,2,8,72]{5,2,4,3,1,0:T(8,128)}, u32[]{:S(2)}) copy-start(f32[1,1,64,2,8,72]{5,2,4,3,1,0:T(8,128)} %get-tuple-element.44) | copy-start | bytes 884740
  676.9 19.4 %all-to-all-start.10 = ((bf16[8,2,128]{2,1,0:T(2,128)(2,1)}), bf16[8,2,128]{2,1,0:T(2,128)(2,1)S(1)}, u32[]{:S(2)}, u32[]{:S(2)}) async-start(bf16[8,2,128]{2,1,0:T(2,128)(2,1)} %reshape.755), calls=%async_computation.10 | async-start | bytes 8192 | tf_op jit(solution)/shard_map/all_to_all | solution.py:139
  694.0 19.7 %copy-start.27 = (f32[8]{0:T(128)S(1)}, f32[8]{0:T(128)}, u32[]{:S(2)}) copy-start(f32[8]{0:T(128)} %copy-done.26) | copy-start | bytes 100
  696.3 14.5 %all-to-all-start.8 = ((bf16[1,1,64,2,1152]{4,3,1,0,2:T(2,128)(2,1)}), bf16[1,1,64,2,1152]{4,3,1,0,2:T(2,128)(2,1)S(1)}, u32[]{:S(2)}, u32[]{:S(2)}) async-start(bf16[1,1,64,2,1152]{4,3,1,0,2:T(2,128)(2,1)} %copy.451), calls=%async_computation.8 | async-start | bytes 589824 | tf_op jit(solution)/shard_map/all_to_all | solution.py:138
  (20 other events, 97.4 us)
Sparse Core Ops, SparseCore 0:
  171.2 146.2 all-gather.6
  350.0 150.5 all-gather.8
  504.1 90.5 all-gather.10
